TPU v7x, 32 devices: a whole 2x2x4 slice. The times are simulated.
32 devices in a mesh: row: 8 (over z, x), col: 2 (over core), rank: 2 (over y).
Axes of the slice: x: 2, y: 2, z: 4, core: 2. Of those that a mesh axis runs over, the one named last changes fastest.
Arguments:
- tensor: bfloat16 [64, 2048, 2048], P(None, 'row', 'col'), may hold values from -6 to 6
- aux_factor: bfloat16 [64, 256], P(None, 'rank'), may hold values from -0.75 to 0.75
- row_factor: bfloat16 [2048, 256], P(('row', 'col'), 'rank'), may hold values from -0.125 to 0.125
- col_factor: bfloat16 [2048, 256], P(('col', 'row'), 'rank'), may hold values from -0.125 to 0.125
Outputs:
- row_result: float32 [2048, 256], P(('row', 'col'), 'rank')
- aux_result: float32 [64, 256], P('row', 'rank')
All inputs are finite; a program needn't handle non-finite values.
Results may differ from a plain program's by a relative error of at most 0.0003.
Values may be sent and summed in bfloat16 or wider, within the bound.
A program may use at most 128 MiB of HBM per device.

v0:
```python
import jax
import jax.numpy as jnp
from jax import lax
from jax.sharding import PartitionSpec as P


def reduce_inner(inner, aux_factor, row_panel):
    aux_panel = aux_factor.astype(jnp.float32)
    aux_count = inner.shape[0]
    row_total = jnp.zeros((inner.shape[1], inner.shape[2]), jnp.float32)
    pieces = []
    for start in range(0, aux_count, 8):
        block = inner[start : start + 8]
        row_total = row_total + jnp.sum(block * aux_panel[start : start + 8][:, None, :], axis=0)
        pieces.append(jnp.sum(block * row_panel[None, :, :], axis=1))
    return (row_total, jnp.concatenate(pieces, axis=0))


def body(tensor, aux_factor, row_factor, col_factor):
    row_panel = lax.all_gather(row_factor, "col", axis=0, tiled=True).astype(jnp.float32)
    width = aux_factor.shape[1]
    aux_count = tensor.shape[0]
    orbits = tensor.shape[1]
    flat = tensor.reshape(aux_count * orbits, tensor.shape[2])
    columns = lax.all_gather(col_factor, "row", axis=0, tiled=True)
    inner = jnp.dot(flat, columns, preferred_element_type=jnp.float32)
    inner = inner.reshape(aux_count, orbits, width)
    row_total, aux_total = reduce_inner(inner, aux_factor, row_panel)
    row_result = lax.psum_scatter(row_total, "col", scatter_dimension=0, tiled=True)
    scattered = lax.psum_scatter(aux_total, "row", scatter_dimension=0, tiled=True)
    aux_result = lax.psum(scattered, "col")
    return (row_result, aux_result)


def solution(mesh):
    return jax.shard_map(
        body,
        mesh=mesh,
        in_specs=(
            P(None, "row", "col"),
            P(None, "rank"),
            P(("row", "col"), "rank"),
            P(("col", "row"), "rank"),
        ),
        out_specs=(P(("row", "col"), "rank"), P("row", "rank")),
        check_vma=False,
    )
```

profile of v0, /device:TPU:0, one launch (start us, length us, event | category | flops | bytes accessed | tf_op | source)
XLA Modules:
  0.0 115.6 jit_solution(7216242594102125668)
XLA Ops:
  7.2 0.0 reduce-scatter.2.cloned.1.call-start
  7.2 0.8 fusion.1
  8.0 32.8 %all_gather.6 = bf16[1024,128]{1,0:T(8,128)(2,1)S(1)} all-gather(bf16[128,128]{1,0:T(8,128)(2,1)} %param.7), channel_id=1, replica_groups=mesh['row'=8,'col'=2,'rank'=2] {'row'}, dimensions={0}, use_global_device_ids=true | all-gather | bytes 294912 | tf_op jit(solution)/shard_map/all_gather | solution.py:25
  40.8 0.0 copy-start.1
  40.8 0.0 copy-start.2
  40.8 14.9 %fusion.2 = f32[16384,128]{1,0:T(8,128)S(1)} fusion(bf16[16384,1024]{1,0:T(8,128)(2,1)} %bitcast.20, bf16[1024,128]{1,0:T(8,128)(2,1)S(1)} %all_gather.6), kind=kOutput, calls=%fused_computation.28 | convolution fusion | flops 4294967296 | bytes 42205184 | tf_op jit(solution)/shard_map/dot_general | solution.py:26
  55.7 0.0 copy-start
  55.7 3.2 %copy-done = f32[16384,128]{1,0:T(8,128)} copy-done((f32[16384,128]{1,0:T(8,128)}, f32[16384,128]{1,0:T(8,128)S(1)}, u32[]{:S(2)}) %copy-start) | copy-done | bytes 8388632
  58.9 0.6 fusion
  59.5 0.2 multiply_reduce_fusion.14
  59.6 0.2 multiply_reduce_fusion.8
  59.8 0.2 multiply_reduce_fusion.10
  59.9 0.2 multiply_reduce_fusion.12
  60.1 0.7 add_add_fusion
  60.8 0.0 reduce-scatter.2.cloned.1.call-update
  60.8 0.0 copy-done.1
  60.8 1.9 %all_gather.7 = bf16[256,128]{1,0:T(8,128)(2,1)S(1)} all-gather(bf16[128,128]{1,0:T(8,128)(2,1)S(1)} %copy-done.1), channel_id=1, replica_groups=mesh['row'=8,'col'=2,'rank'=2] {'col'}, dimensions={0}, use_global_device_ids=true | all-gather | bytes 98304 | tf_op jit(solution)/shard_map/all_gather | solution.py:20
  62.7 4.6 %multiply_reduce_fusion = (f32[8,128]{1,0:T(8,128)S(1)}, f32[8,128]{1,0:T(8,128)S(1)}, f32[8,128]{1,0:T(8,128)S(1)}, f32[8,128]{1,0:T(8,128)S(1)}, f32[8,128]{1,...) fusion(f32[256,128]{1,0:T(8,128)S(1)} %convert_element_type.7, f32[16384,128]{1,0:T(8,128)} %copy-done), kind=kLoop, calls=%fused_computation | loop fusion | flops 4186112 | bytes 8552448 | tf_op jit(solution)/shard_map/reduce_sum | solution.py:15
  67.4 0.0 copy-done.2
  67.4 0.6 dynamic-slice
  68.6 37.1 %all-reduce = f32[64,128]{1,0:T(8,128)S(1)} all-reduce(f32[64,128]{1,0:T(8,128)S(1)} %constant_dynamic-update-slice_fusion), channel_id=3, replica_groups=mesh['row'=8,'col'=2,'rank'=2] {'row'}, use_global_device_ids=true, to_apply=%region_17.0.clone | all-reduce | flops 8192 | bytes 65536
  105.7 3.0 %psum.7 = f32[8,128]{1,0:T(8,128)} all-reduce(f32[8,128]{1,0:T(8,128)S(1)} %constant_dynamic-slice_fusion), channel_id=1, replica_groups=mesh['row'=8,'col'=2,'rank'=2] {'col'}, use_global_device_ids=true, to_apply=%region_18.0 | all-reduce | flops 1024 | bytes 8192 | tf_op jit(solution)/shard_map/psum | solution.py:31
  108.8 0.0 reduce-scatter.2.cloned.1.call-done
  (10 shorter events, 0.0 us)
Async XLA Ops:
  7.2 101.6 %reduce-scatter.2.cloned.1.call-start = ((), (), s32[]{:S(2)}) async-start(), calls=%async_computation.1 | async-start | bytes 196608 | tf_op jit(solution)/shard_map/reduce_scatter | solution.py:29
  40.8 20.1 %copy-start.1 = (bf16[128,128]{1,0:T(8,128)(2,1)S(1)}, bf16[128,128]{1,0:T(8,128)(2,1)}, u32[]{:S(2)}) copy-start(bf16[128,128]{1,0:T(8,128)(2,1)} %param.6) | copy-start | bytes 98308
  40.8 26.6 %copy-start.2 = (u32[32]{0:T(128)S(1)}, u32[32]{0:T(128)}, u32[]{:S(2)}) copy-start(u32[32]{0:T(128)} %constant.4) | copy-start | bytes 388
  55.7 3.2 %copy-start = (f32[16384,128]{1,0:T(8,128)}, f32[16384,128]{1,0:T(8,128)S(1)}, u32[]{:S(2)}) copy-start(f32[16384,128]{1,0:T(8,128)S(1)} %fusion.2) | copy-start | bytes 25165828
Sparse Core Ops, SparseCore 0:
  61.0 8.5 reduce-scatter.1
where the time goes:
time: 116 us
  blocking collectives  74.7 us (64%)
  matrix products  14.9 us (13%)
  between operations  14.8 us (13%)
  other arithmetic  5.94 us (5%)
  local copies, waits for them, and re-layouts  5.2 us (4%)
    unnamed x1, blocking collectives  37.1 us
    all_gather x1, blocking collectives, body(): columns = lax.all_gather(col_factor, 'row', axis=0, tiled=True)  32.8 us
    dot_general x1, matrix products, body(): inner = jnp.dot(flat, columns, preferred_element_type=jnp.float32)  14.9 us
    reduce_sum x1, other arithmetic, reduce_inner(): pieces.append(jnp.sum(block * row_panel[None, :, :], axis=1))  4.59 us
    unnamed x15, local copies, waits for them, and re-layouts  3.83 us
    psum x1, blocking collectives, body(): aux_result = lax.psum(scattered, 'col')  3.04 us
  transfers between devices with their start and end apart: 1, of which 0 were waited for; matrix products, arithmetic and copies ran while one was open for 5% of the time, Pallas kernels for 0%

commit v1 on v0

--- a/solution.py
+++ b/solution.py
@@ -22,7 +22,17 @@
     aux_count = tensor.shape[0]
     orbits = tensor.shape[1]
     flat = tensor.reshape(aux_count * orbits, tensor.shape[2])
-    columns = lax.all_gather(col_factor, "row", axis=0, tiled=True)
+
+    def bench_part(packet, in_dim=0):
+        arr_now = lax.all_to_all(
+            jnp.stack([packet for _ in range(lax.axis_size("row"))], 0),
+            axis_name="row",
+            split_axis=0,
+            concat_axis=0,
+        )
+        return jnp.concatenate(arr_now, in_dim)
+
+    columns = bench_part(col_factor)
     inner = jnp.dot(flat, columns, preferred_element_type=jnp.float32)
     inner = inner.reshape(aux_count, orbits, width)
     row_total, aux_total = reduce_inner(inner, aux_factor, row_panel)

time: 116 us -> 88.4 us (0.76)
  blocking collectives: 74.7 us -> 40.3 us
  starting transfers between devices: 0.04 us -> 7.32 us
  waiting for transfers between devices: 0.02 us -> 4.1 us
  other arithmetic: 5.94 us -> 2.56 us
    all_gather x1 -> x0, blocking collectives: 32.8 us -> none  [body(): columns = lax.all_gather(col_factor, 'row', axis=0, tiled=True)]
    all_to_all x0 -> x1, starting transfers between devices: none -> 7.28 us  [bench_part(): lax.all_to_all(jnp.stack([packet for _ in range(lax.axis_size('row'))], 0...]
    all_to_all x0 -> x1, waiting for transfers between devices: none -> 4.08 us  [bench_part(): lax.all_to_all(jnp.stack([packet for _ in range(lax.axis_size('row'))], 0...]
    reduce_sum x1, other arithmetic: 4.59 us -> 1.22 us  [reduce_inner(): pieces.append(jnp.sum(block * row_panel[None, :, :], axis=1))]
    unnamed x15 -> x9, local copies, waits for them, and re-layouts: 3.83 us -> 1.27 us
    unnamed x1, blocking collectives: 37.1 us -> 35.2 us
    another operation x0 -> x1, local copies, waits for them, and re-layouts: none -> 1.48 us  [bench_part(): jnp.stack([packet for _ in range(lax.axis_size('row'))], 0)]
  transfers between devices with their start and end apart: 1 -> 2, of which waited for: 0 -> 1; matrix products, arithmetic and copies ran while one was open for 5% -> 2% of each run, Pallas kernels for 0% -> 0%
where the time goes in v1:
time: 88.4 us; the launch traced here: 88 us
  blocking collectives  40.3 us (46%)
  matrix products  14.9 us (17%)
  between operations  14.8 us (17%)
  starting transfers between devices  7.32 us (8%)
  local copies, waits for them, and re-layouts  4.13 us (5%)
  waiting for transfers between devices  4.1 us (5%)
  other arithmetic  2.56 us (3%)
    unnamed x1, blocking collectives  35.2 us
    dot_general x1, matrix products, body(): inner = jnp.dot(flat, columns, preferred_element_type=jnp.float32)  14.9 us
    all_to_all x1, starting transfers between devices, bench_part(): lax.all_to_all(jnp.stack([packet for _ in range(lax.axis_size('row'))], 0...  7.28 us
    all_to_all x1, waiting for transfers between devices, bench_part(): lax.all_to_all(jnp.stack([packet for _ in range(lax.axis_size('row'))], 0...  4.08 us
    psum x1, blocking collectives, body(): aux_result = lax.psum(scattered, 'col')  3.04 us
    all_gather x1, blocking collectives, body(): lax.all_gather(row_factor, 'col', axis=0, tiled=True).astype(jnp.float32)  2.07 us
  transfers between devices with their start and end apart: 2, of which 1 were waited for; matrix products, arithmetic and copies ran while one was open for 2% of the time, Pallas kernels for 0%

profile of v1, /device:TPU:0, one launch (start us, length us, event | category | flops | bytes accessed | tf_op | source)
XLA Modules:
  0.0 88.0 jit_solution(16200072867826063831)
XLA Ops:
  7.2 1.5 %stack.2 = bf16[8,128,128]{2,1,0:T(8,128)(2,1)} broadcast(bf16[128,128]{1,0:T(8,128)(2,1)} %param.7), dimensions={1,2} | broadcast | bytes 294912 | tf_op jit(solution)/shard_map/stack | solution.py:28
  8.6 7.3 %all-to-all-start = ((bf16[8,128,128]{2,1,0:T(8,128)(2,1)}), bf16[8,128,128]{2,1,0:T(8,128)(2,1)S(1)}, u32[]{:S(2)}, u32[]{:S(2)}) async-start(bf16[8,128,128]{2,1,0:T(8,128)(2,1)} %stack.2), calls=%async_computation | async-start | bytes 524288 | tf_op jit(solution)/shard_map/all_to_all | solution.py:27
  15.9 0.0 reduce-scatter.2.cloned.1.call-start
  16.0 2.1 %all_gather.3 = bf16[256,128]{1,0:T(8,128)(2,1)S(1)} all-gather(bf16[128,128]{1,0:T(8,128)(2,1)} %param.6), channel_id=1, replica_groups=mesh['row'=8,'col'=2,'rank'=2] {'col'}, dimensions={0}, use_global_device_ids=true | all-gather | bytes 98304 | tf_op jit(solution)/shard_map/all_gather | solution.py:20
  18.1 1.2 %dynamic-slice = u32[1]{0:T(128)} dynamic-slice(u32[32]{0:T(128)} %constant.4, u32[]{:T(128)S(6)} %add.35), dynamic_slice_sizes={1} | dynamic-slice | bytes 12
  20.0 0.8 fusion.1
  20.8 4.1 %all-to-all-done = bf16[8,128,128]{2,1,0:T(8,128)(2,1)S(1)} async-done(((bf16[8,128,128]{2,1,0:T(8,128)(2,1)}), bf16[8,128,128]{2,1,0:T(8,128)(2,1)S(1)}, u32[]{:S(2)}, u32[]{:S(2)}) %all-to-all-start) | async-done | bytes 262176 | tf_op jit(solution)/shard_map/all_to_all | solution.py:27
  24.8 14.9 %fusion.2 = f32[16384,128]{1,0:T(8,128)S(1)} fusion(bf16[16384,1024]{1,0:T(8,128)(2,1)} %bitcast.21, bf16[1024,128]{1,0:T(8,128)(2,1)S(1)} %bitcast.30), kind=kOutput, calls=%fused_computation.28 | convolution fusion | flops 4294967296 | bytes 42205184 | tf_op jit(solution)/shard_map/dot_general | solution.py:36
  39.7 0.6 fusion
  40.3 1.2 %multiply_reduce_fusion = (f32[8,128]{1,0:T(8,128)S(1)}, f32[8,128]{1,0:T(8,128)S(1)}, f32[8,128]{1,0:T(8,128)S(1)}, f32[8,128]{1,0:T(8,128)S(1)}, f32[8,128]{1,...) fusion(f32[256,128]{1,0:T(8,128)S(1)} %convert_element_type.7, ...), kind=kLoop, calls=%fused_computation | loop fusion | flops 4186112 | bytes 8552448 | tf_op jit(solution)/shard_map/reduce_sum | solution.py:15
  41.5 0.2 multiply_reduce_fusion.14
  41.7 0.2 multiply_reduce_fusion.8
  41.9 0.2 multiply_reduce_fusion.10
  42.0 0.2 multiply_reduce_fusion.12
  42.2 0.7 add_add_fusion
  42.9 0.0 reduce-scatter.2.cloned.1.call-update
  43.0 35.2 %all-reduce = f32[64,128]{1,0:T(8,128)S(1)} all-reduce(f32[64,128]{1,0:T(8,128)S(1)} %constant_dynamic-update-slice_fusion), channel_id=3, replica_groups=mesh['row'=8,'col'=2,'rank'=2] {'row'}, use_global_device_ids=true, to_apply=%region_17.0.clone | all-reduce | flops 8192 | bytes 65536
  78.1 3.0 %psum.7 = f32[8,128]{1,0:T(8,128)} all-reduce(f32[8,128]{1,0:T(8,128)S(1)} %constant_dynamic-slice_fusion), channel_id=1, replica_groups=mesh['row'=8,'col'=2,'rank'=2] {'col'}, use_global_device_ids=true, to_apply=%region_18.0 | all-reduce | flops 1024 | bytes 8192 | tf_op jit(solution)/shard_map/psum | solution.py:41
  81.2 0.0 reduce-scatter.2.cloned.1.call-done
  (10 shorter events, 0.0 us)
Async XLA Ops:
  8.6 16.2 %all-to-all-start = ((bf16[8,128,128]{2,1,0:T(8,128)(2,1)}), bf16[8,128,128]{2,1,0:T(8,128)(2,1)S(1)}, u32[]{:S(2)}, u32[]{:S(2)}) async-start(bf16[8,128,128]{2,1,0:T(8,128)(2,1)} %stack.2), calls=%async_computation | async-start | bytes 524288 | tf_op jit(solution)/shard_map/all_to_all | solution.py:27
  15.9 65.2 %reduce-scatter.2.cloned.1.call-start = ((), (), s32[]{:S(2)}) async-start(), calls=%async_computation.2 | async-start | bytes 196608 | tf_op jit(solution)/shard_map/reduce_scatter | solution.py:39
Sparse Core Ops, SparseCore 0:
  43.0 6.5 reduce-scatter.1
